TPU v7x, 32 devices: a whole 2x2x4 slice. The times are simulated.
32 devices in a mesh: dp: 16 (over z, y, core), rows: 2 (over x).
Axes of the slice: x: 2, y: 2, z: 4, core: 2. Of those that a mesh axis runs over, the one named last changes fastest.
Arguments:
- latents: bfloat16 [16, 4, 128, 320], P('dp', 'rows'), may hold values from -6 to 6
- mean_one: float32 [16, 32], P('dp'), may hold values from -0.5 to 0.5
- rstd_one: float32 [16, 32], P('dp'), may hold values from 0.5 to 2
- gain_one: float32 [320], replicated, may hold values from 0.25 to 1.75
- shift_one: float32 [320], replicated, may hold values from -0.5 to 0.5
- kernel_one: bfloat16 [4, 9, 25600], P(None, None, 'dp'), may hold values from -0.109375 to 0.109375
- bias_one: float32 [320], replicated, may hold values from -3 to 3
- embed_bias: float32 [16, 320], P('dp'), may hold values from -3 to 3
- mean_two: float32 [16, 32], P('dp'), may hold values from -0.5 to 0.5
- rstd_two: float32 [16, 32], P('dp'), may hold values from 0.5 to 2
- gain_two: float32 [320], replicated, may hold values from 0.25 to 1.75
- shift_two: float32 [320], replicated, may hold values from -0.5 to 0.5
- kernel_two: bfloat16 [4, 9, 25600], P(None, None, 'dp'), may hold values from -0.109375 to 0.109375
- bias_two: float32 [320], replicated, may hold values from -3 to 3
Outputs:
- block_out: bfloat16 [16, 4, 128, 320], P('dp', 'rows')
All inputs are finite; a program needn't handle non-finite values.
Results may differ from a plain program's by a relative error of at most 0.0045.
Values may be sent and summed in bfloat16 or wider, within the bound.
No kernel may reach another device: no remote copies, remote signals or barrier semaphores. Data moves between devices by JAX's collectives and lax.ppermute only.
A program may use at most 192 MiB of HBM per device.

v0:
```python
import jax
import jax.numpy as jnp
from jax import lax
from jax.sharding import PartitionSpec as P


def padded_2(array, sides, width):
    for axis, dim in sides:
        devices, length = (lax.axis_size(axis), array.shape[dim])
        up = [(i, (i + 1) % devices) for i in range(devices - 1)]
        down = [(j, i) for i, j in up]
        last = lax.slice_in_dim(array, length - width, length, axis=dim)
        first = lax.slice_in_dim(array, 0, width, axis=dim)
        before = lax.ppermute(last, axis, up)
        after = lax.ppermute(first, axis, down)
        array = jnp.concatenate([before, array, after], axis=dim)
    return array


def norm_silu(values, group_mean, group_rstd, gain_vec, shift_vec):
    height, columns, channels = values.shape
    groups = group_mean.shape[-1]
    grouped = values.reshape(height, columns, groups, channels // groups)
    scaled = (grouped - group_mean[0][:, None]) * group_rstd[0][:, None]
    return jax.nn.silu(scaled.reshape(height, columns, channels) * gain_vec + shift_vec)


def padded_rows(activation):
    padded = padded_2(activation, (("rows", 0),), 1)
    return jnp.pad(padded, ((0, 0), (1, 1), (0, 0)))


def window_at(padded, position, height, columns, first_channel, depth):
    tap_row = position // 3
    tap_col = position % 3
    window = padded[
        tap_row : tap_row + height,
        tap_col : tap_col + columns,
        first_channel : first_channel + depth,
    ]
    return window.reshape(height * columns, depth)


def reorder_whole(whole_kernel, channels):
    blocks = whole_kernel.shape[0]
    split = whole_kernel.reshape(blocks, 9, channels // blocks, channels)
    return jnp.transpose(split, (1, 0, 2, 3)).reshape(3, 3 * channels, channels)


def whole_weights(kernel, channels):
    whole_kernel = lax.all_gather(kernel, "dp", axis=2, tiled=True)
    return reorder_whole(whole_kernel, channels)


def convolve_whole(activation, weights):
    height, columns, channels = activation.shape
    padded = padded_rows(activation)
    accumulated = jnp.zeros((height * columns, channels), jnp.float32)
    for tap_row in range(3):
        windows = jnp.concatenate(
            [
                window_at(padded, 3 * tap_row + tap_col, height, columns, 0, channels)
                for tap_col in range(3)
            ],
            axis=1,
        )
        accumulated = accumulated + jnp.dot(
            windows, weights[tap_row], preferred_element_type=jnp.float32
        )
    return accumulated.reshape(height, columns, channels)


def shards(
    latents,
    mean_one,
    rstd_one,
    gain_one,
    shift_one,
    kernel_one,
    bias_one,
    embed_bias,
    mean_two,
    rstd_two,
    gain_two,
    shift_two,
    kernel_two,
    bias_two,
):
    channels = latents.shape[3]
    sample = latents[0].astype(jnp.float32)
    first_act = norm_silu(sample, mean_one, rstd_one, gain_one, shift_one).astype(jnp.bfloat16)
    hidden = (
        convolve_whole(first_act, whole_weights(kernel_one, channels)) + bias_one + embed_bias[0]
    )
    second_act = norm_silu(hidden, mean_two, rstd_two, gain_two, shift_two).astype(jnp.bfloat16)
    result = convolve_whole(second_act, whole_weights(kernel_two, channels)) + bias_two + sample
    return result.astype(jnp.bfloat16)[None]


def solution(mesh):
    placed = (
        P("dp", "rows", None, None),
        P("dp", None),
        P("dp", None),
        P(),
        P(),
        P(None, None, "dp"),
        P(),
        P("dp", None),
        P("dp", None),
        P("dp", None),
        P(),
        P(),
        P(None, None, "dp"),
        P(),
    )
    return jax.shard_map(
        shards, mesh=mesh, in_specs=placed, out_specs=P("dp", "rows", None, None), check_vma=False
    )
```

profile of v0, /device:TPU:0, one launch (start us, length us, event | category | flops | bytes accessed | tf_op | source)
XLA Modules:
  0.0 321.2 jit_solution(16401829512371649083)
XLA Ops:
  6.5 3.1 copy.65
  9.8 2.4 copy.77
  12.9 4.9 %collective-permute-start = (bf16[1,128,320]{1,2,0:T(8,128)(2,1)S(1)}, bf16[1,128,320]{1,2,0:T(8,128)(2,1)S(1)}, u32[]{:S(2)}, u32[]{:S(2)}) collective-permute-start(bf16[1,128,320]{1,2,0:T(8,128)(2,1)S(1)} %get-tuple-element.29), channel_id=1, source_target_pairs={{0,1},{2,3},{4,5},{6,7},{8,9},{10,11},{12,13},{14,15},{16,17},{18,... | collective-permute-start | bytes 245768 | tf_op jit(solution)/shard_map/ppermute | solution.py:14
  17.8 1.3 collective-permute-start.1
  19.3 0.9 multiply_convert_fusion.2
  20.6 3.5 %collective-permute-done.1 = bf16[1,128,320]{1,2,0:T(8,128)(2,1)S(1)} collective-permute-done((bf16[1,128,320]{1,2,0:T(8,128)(2,1)S(1)}, bf16[1,128,320]{1,2,0:T(8,128)(2,1)S(1)}, u32[]{:S(2)}, u32[]{:S(2)}) %collective-permute-start.1) | collective-permute-done | bytes 81952 | tf_op jit(solution)/shard_map/ppermute | solution.py:15
  24.2 0.3 fusion.5
  24.8 0.7 copy_bitcast_fusion.11
  25.5 120.5 %all-gather.3.cloned.1.call-done = bf16[4,9,25600]{1,0,2:T(4,128)(2,1)} async-done(((bf16[4,9,1600]{1,0,2:T(4,128)(2,1)}), bf16[4,9,25600]{1,0,2:T(4,128)(2,1)}) %all-gather.3.cloned.1.call-update) | async-done | bytes 1843216 | tf_op jit(solution)/shard_map/all_gather | solution.py:51
  146.0 30.0 %copy.66 = bf16[4,9,80,320]{3,2,0,1:T(8,128)(2,1)S(1)} copy(bf16[4,9,80,320]{1,0,3,2:T(4,128)(2,1)} %bitcast.136) | data formatting | bytes 3686400 | tf_op jit(solution)/shard_map/reshape | solution.py:46
  176.3 0.4 fusion.6
  176.8 0.4 copy-done.1
  177.3 0.4 convolution_add_fusion.3
  177.8 0.6 multiply_convert_fusion
  178.4 0.3 multiply_convert_fusion.1
  178.8 3.4 %collective-permute-start.2 = (bf16[1,128,320]{1,2,0:T(8,128)(2,1)S(1)}, bf16[1,128,320]{1,2,0:T(8,128)(2,1)S(1)}, u32[]{:S(2)}, u32[]{:S(2)}) collective-permute-start(bf16[1,128,320]{1,2,0:T(8,128)(2,1)S(1)} %get-tuple-element.25), channel_id=1, source_target_pairs={{0,1},{2,3},{4,5},{6,7},{8,9},{10,11},{12,13},{14,15},{16,17},{18,... | collective-permute-start | bytes 245768 | tf_op jit(solution)/shard_map/ppermute | solution.py:14
  182.2 1.3 collective-permute-start.3
  183.5 97.6 %all-gather.5.cloned.1.call-done = bf16[4,9,25600]{1,0,2:T(4,128)(2,1)} async-done(((bf16[4,9,1600]{1,0,2:T(4,128)(2,1)}), bf16[4,9,25600]{1,0,2:T(4,128)(2,1)}) %all-gather.5.cloned.1.call-update) | async-done | bytes 1843216 | tf_op jit(solution)/shard_map/all_gather | solution.py:51
  281.1 29.7 %copy.78 = bf16[4,9,80,320]{3,2,0,1:T(8,128)(2,1)S(1)} copy(bf16[4,9,80,320]{1,0,3,2:T(4,128)(2,1)} %bitcast.135) | data formatting | bytes 3686400 | tf_op jit(solution)/shard_map/reshape | solution.py:46
  311.2 0.3 select_maximum_fusion
  312.0 0.4 fusion.22
  312.4 0.4 convolution_add_fusion.1
  312.9 0.4 convolution_add_fusion
  313.5 0.8 fusion.50
  (67 shorter events, 3.0 us)
Async XLA Ops:
  6.5 3.3 %copy-start.3 = (bf16[4,9,1600]{2,0,1:T(4,128)(2,1)S(1)}, bf16[4,9,1600]{2,0,1:T(4,128)(2,1)}, u32[]{:S(2)}) copy-start(bf16[4,9,1600]{2,0,1:T(4,128)(2,1)} %param.26) | copy-start | bytes 345604
  6.5 139.5 %all-gather.3.cloned.1.call-start = ((), (), s32[]{:S(2)}) async-start(), calls=%async_computation | async-start | bytes 27852800 | tf_op jit(solution)/shard_map/all_gather | solution.py:51
  9.7 2.5 copy-start.11
  9.7 2.7 copy-start.12
  9.7 2.9 copy-start
  9.7 2.9 copy-start.4
  9.7 2.9 copy-start.5
  9.7 271.4 %all-gather.5.cloned.1.call-start = ((), (), s32[]{:S(2)}) async-start(), calls=%async_computation.1 | async-start | bytes 27852800 | tf_op jit(solution)/shard_map/all_gather | solution.py:51
  12.2 8.0 %copy-start.13 = (f32[1,32]{1,0:T(1,128)S(1)}, f32[1,32]{1,0:T(1,128)}, u32[]{:S(2)}) copy-start(f32[1,32]{1,0:T(1,128)} %param.23) | copy-start | bytes 388
  12.2 8.2 %copy-start.14 = (f32[1,32]{1,0:T(1,128)S(1)}, f32[1,32]{1,0:T(1,128)}, u32[]{:S(2)}) copy-start(f32[1,32]{1,0:T(1,128)} %param.22) | copy-start | bytes 388
  12.2 8.4 %copy-start.10 = (f32[1,320]{1,0:T(1,128)S(1)}, f32[1,320]{1,0:T(1,128)}, u32[]{:S(2)}) copy-start(f32[1,320]{1,0:T(1,128)} %param.21) | copy-start | bytes 3844
  12.9 7.7 %collective-permute-start = (bf16[1,128,320]{1,2,0:T(8,128)(2,1)S(1)}, bf16[1,128,320]{1,2,0:T(8,128)(2,1)S(1)}, u32[]{:S(2)}, u32[]{:S(2)}) collective-permute-start(bf16[1,128,320]{1,2,0:T(8,128)(2,1)S(1)} %get-tuple-element.29), channel_id=1, source_target_pairs={{0,1},{2,3},{4,5},{6,7},{8,9},{10,11},{12,13},{14,15},{16,17},{18,... | collective-permute-start | bytes 245768 | tf_op jit(solution)/shard_map/ppermute | solution.py:14
  17.8 6.3 %collective-permute-start.1 = (bf16[1,128,320]{1,2,0:T(8,128)(2,1)S(1)}, bf16[1,128,320]{1,2,0:T(8,128)(2,1)S(1)}, u32[]{:S(2)}, u32[]{:S(2)}) collective-permute-start(bf16[1,128,320]{1,2,0:T(8,128)(2,1)S(1)} %get-tuple-element.30), channel_id=1, source_target_pairs={{1,0},{3,2},{5,4},{7,6},{9,8},{11,10},{13,12},{15,14},{17,16},{19,... | collective-permute-start | bytes 245768 | tf_op jit(solution)/shard_map/ppermute | solution.py:15
  176.3 0.9 copy-start.1
  176.3 1.0 copy-start.2
  176.8 1.0 copy-start.6
  176.8 1.0 copy-start.7
  176.8 1.0 copy-start.8
  178.8 132.3 %collective-permute-start.2 = (bf16[1,128,320]{1,2,0:T(8,128)(2,1)S(1)}, bf16[1,128,320]{1,2,0:T(8,128)(2,1)S(1)}, u32[]{:S(2)}, u32[]{:S(2)}) collective-permute-start(bf16[1,128,320]{1,2,0:T(8,128)(2,1)S(1)} %get-tuple-element.25), channel_id=1, source_target_pairs={{0,1},{2,3},{4,5},{6,7},{8,9},{10,11},{12,13},{14,15},{16,17},{18,... | collective-permute-start | bytes 245768 | tf_op jit(solution)/shard_map/ppermute | solution.py:14
  182.2 128.9 %collective-permute-start.3 = (bf16[1,128,320]{1,2,0:T(8,128)(2,1)S(1)}, bf16[1,128,320]{1,2,0:T(8,128)(2,1)S(1)}, u32[]{:S(2)}, u32[]{:S(2)}) collective-permute-start(bf16[1,128,320]{1,2,0:T(8,128)(2,1)S(1)} %get-tuple-element.26), channel_id=1, source_target_pairs={{1,0},{3,2},{5,4},{7,6},{9,8},{11,10},{13,12},{15,14},{17,16},{19,... | collective-permute-start | bytes 245768 | tf_op jit(solution)/shard_map/ppermute | solution.py:15
  312.9 0.7 copy-start.9
Sparse Core Ops, SparseCore 0:
  9.8 136.1 all-gather.2
  147.6 133.4 all-gather.4
where the time goes:
time: 323 us; the launch traced here: 321 us
  waiting for transfers between devices  222 us (69%)
  local copies, waits for them, and re-layouts  68.9 us (21%)
  between operations  13.9 us (4%)
  starting transfers between devices  10.9 us (3%)
    all_gather x2, waiting for transfers between devices, whole_weights(): whole_kernel = lax.all_gather(kernel, 'dp', axis=2, tiled=True)  218 us
    reshape x2, local copies, waits for them, and re-layouts, reorder_whole(): split = whole_kernel.reshape(blocks, 9, channels // blocks, channels)  59.7 us
    ppermute x2, starting transfers between devices, padded_2(): before = lax.ppermute(last, axis, up)  8.29 us
    unnamed x34, local copies, waits for them, and re-layouts  6.57 us
  transfers between devices with their start and end apart: 6, of which 3 were waited for; matrix products, arithmetic and copies ran while one was open for 21% of the time, Pallas kernels for 0%

commit v1 on v0

--- a/solution.py
+++ b/solution.py
@@ -2,6 +2,18 @@
 import jax.numpy as jnp
 from jax import lax
 from jax.sharding import PartitionSpec as P
+
+
+def doubled_up(x, axis, dim):
+    ways, here, hop = (lax.axis_size(axis), lax.axis_index(axis), x.shape[dim])
+    line, have = (x, 1)
+    while have < ways:
+        line = jnp.concatenate(
+            [line, lax.ppermute(line, axis, [(d, (d - have) % ways) for d in range(ways)])],
+            axis=dim,
+        )
+        have = 2 * have
+    return jnp.roll(line, here * hop, axis=dim)
 
 
 def padded_2(array, sides, width):
@@ -48,7 +60,7 @@
 
 
 def whole_weights(kernel, channels):
-    whole_kernel = lax.all_gather(kernel, "dp", axis=2, tiled=True)
+    whole_kernel = doubled_up(kernel, "dp", 2)
     return reorder_whole(whole_kernel, channels)
 
 

time: 323 us -> 162 us (0.50)
  waiting for transfers between devices: 222 us -> 84.4 us
  local copies, waits for them, and re-layouts: 68.9 us -> 37.6 us
  between operations: 13.9 us -> 0.48 us
  other arithmetic: 2.98 us -> 15.1 us
  starting transfers between devices: 10.9 us -> 21 us
    all_gather x2 -> x0, waiting for transfers between devices: 218 us -> none  [whole_weights(): whole_kernel = lax.all_gather(kernel, 'dp', axis=2, tiled=True)]
    ppermute x0 -> x8, waiting for transfers between devices: none -> 83.3 us  [doubled_up(): lax.ppermute(line, axis, [(d, (d - have) % ways) for d in range(ways)])]
    reshape x2, local copies, waits for them, and re-layouts: 59.7 us -> 6.97 us  [reorder_whole(): split = whole_kernel.reshape(blocks, 9, channels // blocks, channels)]
    concatenate x0 -> x6, local copies, waits for them, and re-layouts: none -> 19.1 us  [doubled_up(): jnp.concatenate([line, lax.ppermute(line, axis, [(d, (d - have) % ways) f...]
    concatenate x0 -> x3, other arithmetic: none -> 11.1 us  [the longest x1 9.07 us: doubled_up(): return jnp.roll(line, here * hop, axis=dim)]
    ppermute x0 -> x8, starting transfers between devices: none -> 10.6 us  [doubled_up(): lax.ppermute(line, axis, [(d, (d - have) % ways) for d in range(ways)])]
    reshape x12, local copies, waits for them, and re-layouts: 1.06 us -> 5.32 us  [window_at(): return window.reshape(height * columns, depth)]
    unnamed x34 -> x46, local copies, waits for them, and re-layouts: 6.57 us -> 2.5 us
  transfers between devices with their start and end apart: 6 -> 12, of which waited for: 3 -> 7; matrix products, arithmetic and copies ran while one was open for 21% -> 19% of each run, Pallas kernels for 0% -> 0%
where the time goes in v1:
time: 162 us; the launch traced here: 161 us
  waiting for transfers between devices  84.4 us (52%)
  local copies, waits for them, and re-layouts  37.6 us (23%)
  starting transfers between devices  21 us (13%)
  other arithmetic  15.1 us (9%)
  matrix products  2.77 us (2%)
    ppermute x8, waiting for transfers between devices, doubled_up(): lax.ppermute(line, axis, [(d, (d - have) % ways) for d in range(ways)])  83.3 us
    concatenate x6, local copies, waits for them, and re-layouts, doubled_up(): jnp.concatenate([line, lax.ppermute(line, axis, [(d, (d - have) % ways) f...  19.1 us
    ppermute x8, starting transfers between devices, doubled_up(): lax.ppermute(line, axis, [(d, (d - have) % ways) for d in range(ways)])  10.6 us
    concatenate x1, other arithmetic, doubled_up(): return jnp.roll(line, here * hop, axis=dim)  9.07 us
    ppermute x2, starting transfers between devices, padded_2(): before = lax.ppermute(last, axis, up)  7.67 us
    reshape x2, local copies, waits for them, and re-layouts, reorder_whole(): split = whole_kernel.reshape(blocks, 9, channels // blocks, channels)  6.97 us
    reshape x12, local copies, waits for them, and re-layouts, window_at(): return window.reshape(height * columns, depth)  5.32 us
  transfers between devices with their start and end apart: 12, of which 7 were waited for; matrix products, arithmetic and copies ran while one was open for 19% of the time, Pallas kernels for 0%

profile of v1, /device:TPU:0, one launch (start us, length us, event | category | flops | bytes accessed | tf_op | source)
XLA Modules:
  0.0 161.3 jit_solution(11446005545301198326)
XLA Ops:
  0.0 5.5 %collective-permute-start.2 = (bf16[4,9,1600]{2,0,1:T(4,128)(2,1)}, bf16[4,9,1600]{2,0,1:T(4,128)(2,1)S(1)}, u32[]{:S(2)}, u32[]{:S(2)}) collective-permute-start(bf16[4,9,1600]{2,0,1:T(4,128)(2,1)} %param.21), channel_id=1, source_target_pairs={{0,30},{2,0},{4,2},{6,4},{8,6},{10,8},{12,10},{14,12},{16,14},{18,... | collective-permute-start | bytes 345608 | tf_op jit(solution)/shard_map/ppermute | solution.py:12
  7.9 1.2 multiply_convert_fusion.3
  9.1 3.4 %collective-permute-start = (bf16[1,128,320]{1,2,0:T(8,128)(2,1)S(1)}, bf16[1,128,320]{1,2,0:T(8,128)(2,1)S(1)}, u32[]{:S(2)}, u32[]{:S(2)}) collective-permute-start(bf16[1,128,320]{1,2,0:T(8,128)(2,1)S(1)} %get-tuple-element.30), channel_id=1, source_target_pairs={{0,1},{2,3},{4,5},{6,7},{8,9},{10,11},{12,13},{14,15},{16,17},{18,... | collective-permute-start | bytes 245768 | tf_op jit(solution)/shard_map/ppermute | solution.py:26
  12.5 1.3 collective-permute-start.1
  17.6 1.5 collective-permute-start.9
  20.4 4.1 %collective-permute-done.3 = bf16[4,9,3200]{2,0,1:T(4,128)(2,1)S(1)} collective-permute-done((bf16[4,9,3200]{2,0,1:T(4,128)(2,1)S(1)}, bf16[4,9,3200]{2,0,1:T(4,128)(2,1)S(1)}, u32[]{:S(2)}, u32[]{:S(2)}) %collective-permute-start.3) | collective-permute-done | bytes 230432 | tf_op jit(solution)/shard_map/ppermute | solution.py:12
  26.1 2.0 %collective-permute-done.9 = bf16[4,9,3200]{2,0,1:T(4,128)(2,1)S(1)} collective-permute-done((bf16[4,9,3200]{2,0,1:T(4,128)(2,1)S(1)}, bf16[4,9,3200]{2,0,1:T(4,128)(2,1)S(1)}, u32[]{:S(2)}, u32[]{:S(2)}) %collective-permute-start.9) | collective-permute-done | bytes 230432 | tf_op jit(solution)/shard_map/ppermute | solution.py:12
  28.1 1.6 concatenate.83
  31.5 7.6 %collective-permute-done.4 = bf16[4,9,6400]{2,0,1:T(4,128)(2,1)S(1)} collective-permute-done((bf16[4,9,6400]{2,0,1:T(4,128)(2,1)S(1)}, bf16[4,9,6400]{2,0,1:T(4,128)(2,1)S(1)}, u32[]{:S(2)}, u32[]{:S(2)}) %collective-permute-start.4) | collective-permute-done | bytes 460832 | tf_op jit(solution)/shard_map/ppermute | solution.py:12
  39.1 1.6 concatenate.74
  40.7 6.7 %collective-permute-done.10 = bf16[4,9,6400]{2,0,1:T(4,128)(2,1)S(1)} collective-permute-done((bf16[4,9,6400]{2,0,1:T(4,128)(2,1)}, bf16[4,9,6400]{2,0,1:T(4,128)(2,1)S(1)}, u32[]{:S(2)}, u32[]{:S(2)}) %collective-permute-start.10) | collective-permute-done | bytes 460832 | tf_op jit(solution)/shard_map/ppermute | solution.py:12
  47.4 2.9 %concatenate.84 = bf16[4,9,12800]{2,0,1:T(4,128)(2,1)} concatenate(bf16[4,9,1600]{2,0,1:T(4,128)(2,1)S(1)} %copy-done.1, bf16[4,9,1600]{2,0,1:T(4,128)(2,1)S(1)} %collective-permute-done.8, bf16[4,9,3200]{2,0,1:T(4,128)(2,1)S(1)} %collective-permute-done.9, bf16[4,9,6400]{2,0,1:T(4,128)(2,1)S(1)} %collective-permute-done.10), dimensions={2} | concatenate | bytes 1843200 | tf_op jit(solution)/shard_map/concatenate | solution.py:11
  50.2 1.3 collective-permute-start.11
  51.6 1.8 %copy_bitcast_fusion.13 = (bf16[256,320]{0,1:T(8,128)(2,1)}, bf16[256,320]{0,1:T(8,128)(2,1)}) fusion(bf16[2,40,8,128]{3,2,1,0:T(8,128)(2,1)} %get-tuple-element.21, bf16[2,40,8,128]{3,2,1,0:T(8,128)(2,1)} %get-tuple-element.22), kind=kLoop, calls=%fused_computation.88 | loop fusion | bytes 655360 | tf_op jit(solution)/shard_map/reshape | solution.py:53
  54.1 1.8 %copy_bitcast_fusion.11 = (bf16[256,320]{0,1:T(8,128)(2,1)}, bf16[256,320]{0,1:T(8,128)(2,1)}) fusion(bf16[2,40,8,128]{3,2,1,0:T(8,128)(2,1)} %get-tuple-element.19, bf16[2,40,8,128]{3,2,1,0:T(8,128)(2,1)} %get-tuple-element.20), kind=kLoop, calls=%fused_computation.86 | loop fusion | bytes 655360 | tf_op jit(solution)/shard_map/reshape | solution.py:53
  56.7 49.8 %collective-permute-done.5 = bf16[4,9,12800]{2,0,1:T(4,128)(2,1)} collective-permute-done((bf16[4,9,12800]{2,0,1:T(4,128)(2,1)S(1)}, bf16[4,9,12800]{2,0,1:T(4,128)(2,1)}, u32[]{:S(2)}, u32[]{:S(2)}) %collective-permute-start.5) | collective-permute-done | bytes 921632 | tf_op jit(solution)/shard_map/ppermute | solution.py:12
  106.5 5.4 %concatenate.75 = bf16[4,9,25600]{2,0,1:T(4,128)(2,1)S(1)} concatenate(bf16[4,9,1600]{2,0,1:T(4,128)(2,1)S(1)} %copy-done, bf16[4,9,1600]{2,0,1:T(4,128)(2,1)S(1)} %collective-permute-done.2, bf16[4,9,3200]{2,0,1:T(4,128)(2,1)S(1)} %collective-permute-done.3, bf16[4,9,6400]{2,0,1:T(4,128)(2,1)S(1)} %collective-permute-done.4, bf16[4,9,12800]{2,0,1:T(4,128)(2,1)} %collective-permute-done.5), dimensions={2} | concatenate | bytes 3686400 | tf_op jit(solution)/shard_map/concatenate | solution.py:11
  111.9 13.0 %collective-permute-done.11 = bf16[4,9,12800]{2,0,1:T(4,128)(2,1)} collective-permute-done((bf16[4,9,12800]{2,0,1:T(4,128)(2,1)}, bf16[4,9,12800]{2,0,1:T(4,128)(2,1)}, u32[]{:S(2)}, u32[]{:S(2)}) %collective-permute-start.11) | collective-permute-done | bytes 921632 | tf_op jit(solution)/shard_map/ppermute | solution.py:12
  125.0 6.6 %concatenate.85 = bf16[4,9,25600]{2,0,1:T(4,128)(2,1)} concatenate(bf16[4,9,1600]{2,0,1:T(4,128)(2,1)S(1)} %copy-done.1, bf16[4,9,1600]{2,0,1:T(4,128)(2,1)S(1)} %collective-permute-done.8, bf16[4,9,3200]{2,0,1:T(4,128)(2,1)S(1)} %collective-permute-done.9, bf16[4,9,6400]{2,0,1:T(4,128)(2,1)} %copy-done.2, bf16[4,9,12800]{2,0,1:T(4,128)(2,1)} %collective-permute-done.11), dimensions={2} | concatenate | bytes 3686400 | tf_op jit(solution)/shard_map/concatenate | solution.py:11
  131.5 9.1 %fusion = (bf16[4,9,25600]{2,0,1:T(4,128)(2,1)}, bf16[4,9,25600]{2,0,1:T(4,128)(2,1)}) fusion(s32[]{:T(128)S(6)} %select_n.13, bf16[4,9,25600]{2,0,1:T(4,128)(2,1)} %concatenate.85, bf16[4,9,25600]{2,0,1:T(4,128)(2,1)S(1)} %concatenate.75), kind=kLoop, calls=%fused_computation.6 | loop fusion | flops 7372800 | bytes 7372804 | tf_op jit(solution)/shard_map/jit(_roll_dynamic)/concatenate | solution.py:16
  140.6 3.5 %reshape.125 = bf16[4,9,80,320]{3,2,0,1:T(8,128)(2,1)S(1)} reshape(bf16[4,9,25600]{2,0,1:T(4,128)(2,1)} %get-tuple-element.35) | data formatting | bytes 3686400 | tf_op jit(solution)/shard_map/reshape | solution.py:58
  147.2 4.3 %collective-permute-start.6 = (bf16[1,128,320]{1,2,0:T(8,128)(2,1)S(1)}, bf16[1,128,320]{1,2,0:T(8,128)(2,1)S(1)}, u32[]{:S(2)}, u32[]{:S(2)}) collective-permute-start(bf16[1,128,320]{1,2,0:T(8,128)(2,1)S(1)} %get-tuple-element.26), channel_id=1, source_target_pairs={{0,1},{2,3},{4,5},{6,7},{8,9},{10,11},{12,13},{14,15},{16,17},{18,... | collective-permute-start | bytes 245768 | tf_op jit(solution)/shard_map/ppermute | solution.py:26
  151.5 1.5 collective-permute-start.7
  153.0 3.5 %reshape.135 = bf16[4,9,80,320]{3,2,0,1:T(8,128)(2,1)S(1)} reshape(bf16[4,9,25600]{2,0,1:T(4,128)(2,1)} %get-tuple-element.34) | data formatting | bytes 3686400 | tf_op jit(solution)/shard_map/reshape | solution.py:58
  (98 shorter events, 20.0 us)
Async XLA Ops:
  0.0 24.5 %copy-start = (bf16[4,9,1600]{2,0,1:T(4,128)(2,1)S(1)}, bf16[4,9,1600]{2,0,1:T(4,128)(2,1)}, u32[]{:S(2)}) copy-start(bf16[4,9,1600]{2,0,1:T(4,128)(2,1)} %param.21) | copy-start | bytes 345604
  0.0 19.0 %copy-start.14 = (f32[320]{0:T(512)S(1)}, f32[320]{0:T(512)}, u32[]{:S(2)}) copy-start(f32[320]{0:T(512)} %param.19) | copy-start | bytes 3844
  0.0 19.0 %copy-start.13 = (f32[320]{0:T(512)S(1)}, f32[320]{0:T(512)}, u32[]{:S(2)}) copy-start(f32[320]{0:T(512)} %param.20) | copy-start | bytes 3844
  0.0 20.0 %copy-start.20 = (f32[1,32]{1,0:T(1,128)S(1)}, f32[1,32]{1,0:T(1,128)}, u32[]{:S(2)}) copy-start(f32[1,32]{1,0:T(1,128)} %param.25) | copy-start | bytes 388
  0.0 20.2 %copy-start.21 = (f32[1,32]{1,0:T(1,128)S(1)}, f32[1,32]{1,0:T(1,128)}, u32[]{:S(2)}) copy-start(f32[1,32]{1,0:T(1,128)} %param.24) | copy-start | bytes 388
  0.0 20.3 %copy-start.19 = (f32[1,320]{1,0:T(1,128)S(1)}, f32[1,320]{1,0:T(1,128)}, u32[]{:S(2)}) copy-start(f32[1,320]{1,0:T(1,128)} %param.23) | copy-start | bytes 3844
  0.0 14.9 %collective-permute-start.2 = (bf16[4,9,1600]{2,0,1:T(4,128)(2,1)}, bf16[4,9,1600]{2,0,1:T(4,128)(2,1)S(1)}, u32[]{:S(2)}, u32[]{:S(2)}) collective-permute-start(bf16[4,9,1600]{2,0,1:T(4,128)(2,1)} %param.21), channel_id=1, source_target_pairs={{0,30},{2,0},{4,2},{6,4},{8,6},{10,8},{12,10},{14,12},{16,14},{18,... | collective-permute-start | bytes 345608 | tf_op jit(solution)/shard_map/ppermute | solution.py:12
  5.6 11.0 %collective-permute-start.8 = (bf16[4,9,1600]{2,0,1:T(4,128)(2,1)}, bf16[4,9,1600]{2,0,1:T(4,128)(2,1)S(1)}, u32[]{:S(2)}, u32[]{:S(2)}) collective-permute-start(bf16[4,9,1600]{2,0,1:T(4,128)(2,1)} %param.28), channel_id=1, source_target_pairs={{0,30},{2,0},{4,2},{6,4},{8,6},{10,8},{12,10},{14,12},{16,14},{18,... | collective-permute-start | bytes 345608 | tf_op jit(solution)/shard_map/ppermute | solution.py:12
  7.0 21.1 %copy-start.1 = (bf16[4,9,1600]{2,0,1:T(4,128)(2,1)S(1)}, bf16[4,9,1600]{2,0,1:T(4,128)(2,1)}, u32[]{:S(2)}) copy-start(bf16[4,9,1600]{2,0,1:T(4,128)(2,1)} %param.28) | copy-start | bytes 345604
  9.1 21.0 %collective-permute-start = (bf16[1,128,320]{1,2,0:T(8,128)(2,1)S(1)}, bf16[1,128,320]{1,2,0:T(8,128)(2,1)S(1)}, u32[]{:S(2)}, u32[]{:S(2)}) collective-permute-start(bf16[1,128,320]{1,2,0:T(8,128)(2,1)S(1)} %get-tuple-element.30), channel_id=1, source_target_pairs={{0,1},{2,3},{4,5},{6,7},{8,9},{10,11},{12,13},{14,15},{16,17},{18,... | collective-permute-start | bytes 245768 | tf_op jit(solution)/shard_map/ppermute | solution.py:26
  12.5 17.6 %collective-permute-start.1 = (bf16[1,128,320]{1,2,0:T(8,128)(2,1)S(1)}, bf16[1,128,320]{1,2,0:T(8,128)(2,1)S(1)}, u32[]{:S(2)}, u32[]{:S(2)}) collective-permute-start(bf16[1,128,320]{1,2,0:T(8,128)(2,1)S(1)} %get-tuple-element.31), channel_id=1, source_target_pairs={{1,0},{3,2},{5,4},{7,6},{9,8},{11,10},{13,12},{15,14},{17,16},{19,... | collective-permute-start | bytes 245768 | tf_op jit(solution)/shard_map/ppermute | solution.py:27
  16.0 8.5 %collective-permute-start.3 = (bf16[4,9,3200]{2,0,1:T(4,128)(2,1)S(1)}, bf16[4,9,3200]{2,0,1:T(4,128)(2,1)S(1)}, u32[]{:S(2)}, u32[]{:S(2)}) collective-permute-start(bf16[4,9,3200]{2,0,1:T(4,128)(2,1)S(1)} %pad_maximum_fusion), channel_id=1, source_target_pairs={{0,28},{2,30},{4,0},{6,2},{8,4},{10,6},{12,8},{14,10},{16,12},{18,... | collective-permute-start | bytes 691208 | tf_op jit(solution)/shard_map/ppermute | solution.py:12
  17.6 10.5 %collective-permute-start.9 = (bf16[4,9,3200]{2,0,1:T(4,128)(2,1)S(1)}, bf16[4,9,3200]{2,0,1:T(4,128)(2,1)S(1)}, u32[]{:S(2)}, u32[]{:S(2)}) collective-permute-start(bf16[4,9,3200]{2,0,1:T(4,128)(2,1)S(1)} %pad_maximum_fusion.1), channel_id=1, source_target_pairs={{0,28},{2,30},{4,0},{6,2},{8,4},{10,6},{12,8},{14,10},{16,12},{18,... | collective-permute-start | bytes 691208 | tf_op jit(solution)/shard_map/ppermute | solution.py:12
  25.6 13.5 %collective-permute-start.4 = (bf16[4,9,6400]{2,0,1:T(4,128)(2,1)S(1)}, bf16[4,9,6400]{2,0,1:T(4,128)(2,1)S(1)}, u32[]{:S(2)}, u32[]{:S(2)}) collective-permute-start(bf16[4,9,6400]{2,0,1:T(4,128)(2,1)S(1)} %concatenate.73), channel_id=1, source_target_pairs={{0,24},{2,26},{4,28},{6,30},{8,0},{10,2},{12,4},{14,6},{16,8},{18,... | collective-permute-start | bytes 1382408 | tf_op jit(solution)/shard_map/ppermute | solution.py:12
  29.7 17.7 %collective-permute-start.10 = (bf16[4,9,6400]{2,0,1:T(4,128)(2,1)}, bf16[4,9,6400]{2,0,1:T(4,128)(2,1)S(1)}, u32[]{:S(2)}, u32[]{:S(2)}) collective-permute-start(bf16[4,9,6400]{2,0,1:T(4,128)(2,1)} %concatenate.83), channel_id=1, source_target_pairs={{0,24},{2,26},{4,28},{6,30},{8,0},{10,2},{12,4},{14,6},{16,8},{18,... | collective-permute-start | bytes 1382408 | tf_op jit(solution)/shard_map/ppermute | solution.py:12
  40.7 65.8 %collective-permute-start.5 = (bf16[4,9,12800]{2,0,1:T(4,128)(2,1)S(1)}, bf16[4,9,12800]{2,0,1:T(4,128)(2,1)}, u32[]{:S(2)}, u32[]{:S(2)}) collective-permute-start(bf16[4,9,12800]{2,0,1:T(4,128)(2,1)S(1)} %concatenate.74), channel_id=1, source_target_pairs={{0,16},{2,18},{4,20},{6,22},{8,24},{10,26},{12,28},{14,30},{16,0},... | collective-permute-start | bytes 2764808 | tf_op jit(solution)/shard_map/ppermute | solution.py:12
  47.4 8.5 %copy-start.2 = (bf16[4,9,6400]{2,0,1:T(4,128)(2,1)}, bf16[4,9,6400]{2,0,1:T(4,128)(2,1)S(1)}, u32[]{:S(2)}) copy-start(bf16[4,9,6400]{2,0,1:T(4,128)(2,1)S(1)} %collective-permute-done.10) | copy-start | bytes 1382404
  50.2 74.7 %collective-permute-start.11 = (bf16[4,9,12800]{2,0,1:T(4,128)(2,1)}, bf16[4,9,12800]{2,0,1:T(4,128)(2,1)}, u32[]{:S(2)}, u32[]{:S(2)}) collective-permute-start(bf16[4,9,12800]{2,0,1:T(4,128)(2,1)} %concatenate.84), channel_id=1, source_target_pairs={{0,16},{2,18},{4,20},{6,22},{8,24},{10,26},{12,28},{14,30},{16,0},... | collective-permute-start | bytes 2764808 | tf_op jit(solution)/shard_map/ppermute | solution.py:12
  144.4 1.3 copy-start.10
  144.4 1.3 copy-start.11
  144.4 1.3 copy-start.12
  145.2 1.1 copy-start.15
  147.2 9.5 %collective-permute-start.6 = (bf16[1,128,320]{1,2,0:T(8,128)(2,1)S(1)}, bf16[1,128,320]{1,2,0:T(8,128)(2,1)S(1)}, u32[]{:S(2)}, u32[]{:S(2)}) collective-permute-start(bf16[1,128,320]{1,2,0:T(8,128)(2,1)S(1)} %get-tuple-element.26), channel_id=1, source_target_pairs={{0,1},{2,3},{4,5},{6,7},{8,9},{10,11},{12,13},{14,15},{16,17},{18,... | collective-permute-start | bytes 245768 | tf_op jit(solution)/shard_map/ppermute | solution.py:26
  151.5 6.3 %collective-permute-start.7 = (bf16[1,128,320]{1,2,0:T(8,128)(2,1)S(1)}, bf16[1,128,320]{1,2,0:T(8,128)(2,1)S(1)}, u32[]{:S(2)}, u32[]{:S(2)}) collective-permute-start(bf16[1,128,320]{1,2,0:T(8,128)(2,1)S(1)} %get-tuple-element.27), channel_id=1, source_target_pairs={{1,0},{3,2},{5,4},{7,6},{9,8},{11,10},{13,12},{15,14},{17,16},{19,... | collective-permute-start | bytes 245768 | tf_op jit(solution)/shard_map/ppermute | solution.py:27
  (10 other events, 10.0 us)
